TPU v7x, 32 devices: a whole 2x2x4 slice. The times are simulated.
32 devices in a mesh: row: 4 (over z), col: 8 (over y, x, core).
Axes of the slice: x: 2, y: 2, z: 4, core: 2. Of those that a mesh axis runs over, the one named last changes fastest.
Arguments:
- base_flat: bfloat16 [2, 29568, 8192], P(None, ('row', 'col')), may hold values from -6 to 6
- adjusted_flat: bfloat16 [2, 29568, 8192], P(None, ('row', 'col')), may hold values from -6 to 6
- omega: bfloat16 [2, 8192, 256], P(None, 'col'), may hold values from -6 to 6
Outputs:
- adapter_up_basis: float32 [2, 29568, 256], P(None, ('row', 'col'))
- adapter_down_transposed: float32 [2, 8192, 256], P(None, 'col', 'row')
All inputs are finite; a program needn't handle non-finite values.
Results may differ from a plain program's by a relative error of at most 0.011.
Values may be sent and summed in bfloat16 or wider, within the bound.
No kernel may reach another device: no remote copies, remote signals or barrier semaphores. Data moves between devices by JAX's collectives and lax.ppermute only.
A program may use at most 192 MiB of HBM per device.

v0:
```python
import math
import jax
import jax.numpy as jnp
from jax import lax
from jax.sharding import PartitionSpec as P

HIDDEN_UNITS = 29568


def sketch_term(blocks, right):
    terms = []
    for index in range(blocks.shape[0]):
        rows = blocks[index]
        terms.append(jnp.dot(rows, right[index], preferred_element_type=jnp.float32))
    return jnp.concatenate(terms, axis=1)


def gram_of(panel, matrix_list, adapter_rank):
    panel_three = panel.reshape(panel.shape[0], matrix_list, adapter_rank)
    return jnp.einsum("rmk,rml->mkl", panel_three, panel_three, precision=lax.Precision.HIGHEST)


def orthonormal(panel, gram_total, matrix_list, adapter_rank):
    lower = jnp.linalg.cholesky(gram_total)
    stacked = panel.reshape(panel.shape[0], matrix_list, adapter_rank).transpose(1, 2, 0)
    solved = jax.scipy.linalg.solve_triangular(lower, stacked, lower=True)
    return solved.transpose(2, 0, 1).reshape(panel.shape[0], matrix_list * adapter_rank)


def contract(total, blocks, piece):
    adapter_rank = total.shape[2]
    terms = []
    for index in range(blocks.shape[0]):
        rows = blocks[index]
        terms.append(
            lax.dot_general(
                rows,
                piece[:, index * adapter_rank : (index + 1) * adapter_rank],
                (((0,), (0,)), ((), ())),
                preferred_element_type=jnp.float32,
            )
        )
    return jnp.stack(terms)


def local(base_flat, adjusted_flat, omega):
    matrix_list = base_flat.shape[0]
    adapter_rank = omega.shape[2]
    delta = (adjusted_flat.astype(jnp.float32) - base_flat.astype(jnp.float32)).astype(jnp.bfloat16)
    blocks = lax.all_to_all(delta, "col", split_axis=2, concat_axis=1, tiled=True)
    block_rows = blocks.shape[1]
    block_cols = blocks.shape[2]
    segment_rows = block_rows // lax.axis_size("col")
    col_index = lax.axis_index("col")
    empty = jnp.zeros((matrix_list, block_cols, adapter_rank), jnp.float32)

    def find_basis(right):
        panel = lax.psum(sketch_term(blocks, right), "col")
        gram_total = lax.psum(gram_of(panel, matrix_list, adapter_rank), "row")
        basis = orthonormal(panel, gram_total, matrix_list, adapter_rank)
        own_rows = lax.dynamic_slice_in_dim(basis, col_index * segment_rows, segment_rows, 0)
        folded = contract(empty, blocks, basis.astype(jnp.bfloat16))
        return (own_rows, folded)

    first_rows, first_folded = find_basis(omega)
    shares = lax.psum_scatter(first_folded, "row", scatter_dimension=1, tiled=True)
    columns = lax.all_gather(shares.astype(jnp.bfloat16), "row", axis=1, tiled=True)
    last_basis_rows, last_folded_rows = find_basis(columns)
    adapter_down_transposed = lax.psum_scatter(
        last_folded_rows.astype(jnp.bfloat16), "row", scatter_dimension=2, tiled=True
    ).astype(jnp.float32)
    adapter_up_basis = (
        (math.sqrt(HIDDEN_UNITS) * last_basis_rows)
        .reshape(segment_rows, matrix_list, adapter_rank)
        .transpose(1, 0, 2)
    )
    return (adapter_up_basis, adapter_down_transposed)


def solution(mesh):
    in_specs = (P(None, ("row", "col"), None), P(None, ("row", "col"), None), P(None, "col", None))
    out_specs = (P(None, ("row", "col"), None), P(None, "col", "row"))
    return jax.shard_map(local, mesh=mesh, in_specs=in_specs, out_specs=out_specs, check_vma=False)
```

profile of v0, /device:TPU:0, one launch (start us, length us, event | category | flops | bytes accessed | tf_op | source)
XLA Modules:
  0.0 1735.4 jit_solution(16130789027910597710)
XLA Ops:
  7.2 31.4 %subtract_convert_fusion = bf16[2,924,8192]{2,1,0:T(8,128)(2,1)} fusion(bf16[2,924,8192]{2,0,1:T(2,128)(2,1)} %param.6, bf16[2,924,8192]{2,0,1:T(2,128)(2,1)} %param.7), kind=kLoop, calls=%fused_computation.4 | loop fusion | flops 60555264 | bytes 90832896 | tf_op jit(solution)/shard_map/convert_element_type | solution.py:49
  38.6 82.0 %copy.117 = bf16[2,924,8192]{1,0,2:T(2,128)(2,1)} copy(bf16[2,924,8192]{2,1,0:T(8,128)(2,1)} %subtract_convert_fusion) | data formatting | bytes 60555264 | tf_op jit(solution)/shard_map/convert_element_type | solution.py:49
  120.7 375.5 %all_to_all.15 = bf16[2,924,8192]{1,0,2:T(2,128)(2,1)} all-to-all(bf16[2,924,8192]{1,0,2:T(2,128)(2,1)} %copy.117), channel_id=1, replica_groups=mesh['row'=4,'col'=8] {'col'}, dimensions={2} | all-to-all | bytes 60555264 | tf_op jit(solution)/shard_map/all_to_all | solution.py:50
  496.2 80.7 %copy.118 = bf16[2,924,8,1024]{3,1,2,0:T(8,128)(2,1)} copy(bf16[2,924,8,1024]{1,0,3,2:T(2,128)(2,1)} %bitcast.130) | data formatting | bytes 60555264 | tf_op jit(solution)/shard_map/all_to_all | solution.py:50
  576.9 21.5 %fusion.53 = (bf16[1,8,924,1024]{3,2,1,0:T(8,128)(2,1)}, bf16[1,8,924,1024]{3,2,1,0:T(8,128)(2,1)}) fusion(bf16[2,8,924,1024]{3,2,1,0:T(8,128)(2,1)} %bitcast.131), kind=kLoop, calls=%fused_computation.89 | loop fusion | bytes 60555264 | tf_op jit(solution)/shard_map/slice | solution.py:13
  598.3 11.5 squeeze.26
  609.8 11.6 squeeze.24
  637.5 9.5 pad_maximum_fusion
  647.1 11.8 copy.165
  658.9 200.5 %all-reduce.8.cloned.1.call-done = f32[7392,2,256]{2,0,1:T(8,128)} async-done(((f32[7392,2,256]{2,0,1:T(8,128)}), f32[7392,2,256]{2,0,1:T(8,128)}) %all-reduce.8.cloned.1.call-update) | async-done | bytes 15138832 | tf_op jit(solution)/shard_map/psum | solution.py:58
  859.5 31.0 %fusion.54 = f32[2,256,256]{1,2,0:T(8,128)} fusion(f32[7392,2,256]{2,0,1:T(8,128)} %all-reduce.8.cloned.1.call-done), kind=kOutput, calls=%fused_computation.90 | convolution fusion | flops 11626610688 | bytes 15663104 | tf_op jit(solution)/shard_map/rmk,rml->mkl/dot_general | solution.py:20
  890.6 38.5 %all-reduce.10.cloned.1.call-done = f32[2,256,256]{1,2,0:T(8,128)} async-done(((f32[2,256,256]{1,2,0:T(8,128)}), f32[2,256,256]{1,2,0:T(8,128)}) %all-reduce.10.cloned.1.call-update) | async-done | bytes 524304 | tf_op jit(solution)/shard_map/psum | solution.py:59
  931.5 23.5 %custom-call.17 = f32[2,128,128]{2,1,0:T(8,128)S(1)} custom-call(f32[2,128,128]{2,1,0:T(8,128)S(1)} %cholesky.198), custom_call_target="Cholesky" | custom-call | tf_op jit(solution)/shard_map/jit(cholesky)/cholesky | solution.py:24
  955.0 19.7 %custom-call.18 = f32[2,1,128,128]{2,3,1,0:T(8,128)S(1)} custom-call(f32[2,1,128,128]{3,2,1,0:T(8,128)S(1)} %select_bitcast_fusion.1), custom_call_target="InvertDiagBlocksLowerTriangular" | custom-call | tf_op jit(solution)/shard_map/jit(cholesky)/cholesky | solution.py:24
  975.4 23.5 %custom-call.19 = f32[2,128,128]{2,1,0:T(8,128)S(1)} custom-call(f32[2,128,128]{2,1,0:T(8,128)S(1)} %convolution_subtract_fusion.3), custom_call_target="Cholesky" | custom-call | tf_op jit(solution)/shard_map/jit(cholesky)/cholesky | solution.py:24
  1003.3 39.3 %custom-call.20 = f32[2,2,128,128]{2,3,1,0:T(8,128)S(1)} custom-call(f32[2,2,128,128]{3,2,1,0:T(8,128)S(1)} %bitcast.144), custom_call_target="InvertDiagBlocksLowerTriangular" | custom-call | tf_op jit(solution)/shard_map/jit(_solve_triangular)/vmap()/triangular_solve | solution.py:26
  1074.0 10.2 copy.127
  1102.9 43.5 %reduce-scatter.2.cloned.1.call-done = f32[2,256,256]{2,1,0:T(8,128)} async-done(((f32[2,1024,256]{2,1,0:T(8,128)}), f32[2,256,256]{2,1,0:T(8,128)}) %reduce-scatter.2.cloned.1.call-update) | async-done | bytes 524304 | tf_op jit(solution)/shard_map/reduce_scatter | solution.py:66
  1148.2 27.4 %all-gather.2.cloned.1.call-done = bf16[2,1024,256]{2,1,0:T(8,128)(2,1)} async-done(((bf16[2,256,256]{2,1,0:T(8,128)(2,1)}), bf16[2,1024,256]{2,1,0:T(8,128)(2,1)}) %all-gather.2.cloned.1.call-update) | async-done | bytes 1048592 | tf_op jit(solution)/shard_map/all_gather | solution.py:67
  1175.6 9.8 fusion.32
  1199.0 11.8 copy.164
  1210.8 199.8 %all-reduce.12.cloned.1.call-done = f32[7392,2,256]{2,0,1:T(8,128)} async-done(((f32[7392,2,256]{2,0,1:T(8,128)}), f32[7392,2,256]{2,0,1:T(8,128)}) %all-reduce.12.cloned.1.call-update) | async-done | bytes 15138832 | tf_op jit(solution)/shard_map/psum | solution.py:58
  1410.7 30.9 %fusion.55 = f32[2,256,256]{1,2,0:T(8,128)} fusion(f32[7392,2,256]{2,0,1:T(8,128)} %all-reduce.12.cloned.1.call-done), kind=kOutput, calls=%fused_computation.91 | convolution fusion | flops 11626610688 | bytes 15663104 | tf_op jit(solution)/shard_map/rmk,rml->mkl/dot_general | solution.py:20
  1441.7 38.6 %all-reduce.14.cloned.1.call-done = f32[2,256,256]{1,2,0:T(8,128)} async-done(((f32[2,256,256]{1,2,0:T(8,128)}), f32[2,256,256]{1,2,0:T(8,128)}) %all-reduce.14.cloned.1.call-update) | async-done | bytes 524304 | tf_op jit(solution)/shard_map/psum | solution.py:59
  1482.7 23.5 %custom-call.21 = f32[2,128,128]{2,1,0:T(8,128)S(1)} custom-call(f32[2,128,128]{2,1,0:T(8,128)S(1)} %cholesky.201), custom_call_target="Cholesky" | custom-call | tf_op jit(solution)/shard_map/jit(cholesky)/cholesky | solution.py:24
  1506.2 19.7 %custom-call.22 = f32[2,1,128,128]{2,3,1,0:T(8,128)S(1)} custom-call(f32[2,1,128,128]{3,2,1,0:T(8,128)S(1)} %select_bitcast_fusion), custom_call_target="InvertDiagBlocksLowerTriangular" | custom-call | tf_op jit(solution)/shard_map/jit(cholesky)/cholesky | solution.py:24
  1526.5 23.5 %custom-call.23 = f32[2,128,128]{2,1,0:T(8,128)S(1)} custom-call(f32[2,128,128]{2,1,0:T(8,128)S(1)} %convolution_subtract_fusion.2), custom_call_target="Cholesky" | custom-call | tf_op jit(solution)/shard_map/jit(cholesky)/cholesky | solution.py:24
  1554.5 39.3 %custom-call.24 = f32[2,2,128,128]{2,3,1,0:T(8,128)S(1)} custom-call(f32[2,2,128,128]{3,2,1,0:T(8,128)S(1)} %bitcast.143), custom_call_target="InvertDiagBlocksLowerTriangular" | custom-call | tf_op jit(solution)/shard_map/jit(_solve_triangular)/vmap()/triangular_solve | solution.py:26
  1617.5 11.5 maximum_bitcast_fusion
  1629.0 15.4 copy.136
  1653.6 10.7 fusion.28
  1680.2 46.0 %all-reduce.16.cloned.1.call-done = bf16[2,1024,256]{1,0,2:T(2,128)(2,1)} async-done(((bf16[2,1024,256]{1,0,2:T(2,128)(2,1)}), bf16[2,1024,256]{1,0,2:T(2,128)(2,1)}) %all-reduce.16.cloned.1.call-update) | async-done | bytes 1048592
  (111 shorter events, 154.8 us)
Async XLA Ops:
  7.2 852.3 %all-reduce.8.cloned.1.call-start = ((), (), s32[]{:S(2)}) async-start(), calls=%async_computation.2 | async-start | bytes 30277632 | tf_op jit(solution)/shard_map/psum | solution.py:58
  609.8 11.6 copy-start.7
  621.4 9.6 copy-start.4
  658.9 270.3 %all-reduce.10.cloned.1.call-start = ((), (), s32[]{:S(2)}) async-start(), calls=%async_computation.3 | async-start | bytes 1048576 | tf_op jit(solution)/shard_map/psum | solution.py:59
  890.5 255.9 %reduce-scatter.2.cloned.1.call-start = ((), (), s32[]{:S(2)}) async-start(), calls=%async_computation.4 | async-start | bytes 2621440 | tf_op jit(solution)/shard_map/reduce_scatter | solution.py:66
  1042.6 8.9 copy-start
  1051.5 6.7 copy-start.2
  1084.2 9.0 slice-start
  1084.2 9.8 copy-start.6
  1084.2 11.0 slice-start.1
  1084.2 12.2 slice-start.2
  1084.2 12.9 slice-start.3
  1102.8 72.8 %all-gather.2.cloned.1.call-start = ((), (), s32[]{:S(2)}) async-start(), calls=%async_computation.5 | async-start | bytes 1310720 | tf_op jit(solution)/shard_map/all_gather | solution.py:67
  1148.2 262.5 %all-reduce.12.cloned.1.call-start = ((), (), s32[]{:S(2)}) async-start(), calls=%async_computation.6 | async-start | bytes 30277632 | tf_op jit(solution)/shard_map/psum | solution.py:58
  1175.6 9.8 copy-start.8
  1210.8 269.5 %all-reduce.14.cloned.1.call-start = ((), (), s32[]{:S(2)}) async-start(), calls=%async_computation.7 | async-start | bytes 1048576 | tf_op jit(solution)/shard_map/psum | solution.py:59
  1441.6 284.7 %all-reduce.16.cloned.1.call-start = ((), (), s32[]{:S(2)}) async-start(), calls=%async_computation.8 | async-start | bytes 2097152
  1593.8 8.9 copy-start.1
  1602.7 6.7 copy-start.3
  1653.6 10.7 copy-start.5
  1664.3 10.2 copy-start.9
Sparse Core Ops, SparseCore 0:
  659.0 200.4 all-reduce.7
  890.6 38.4 all-reduce.9
  1102.9 43.4 reduce-scatter.1
  1148.4 27.1 all-gather.1
  1210.9 199.7 all-reduce.11
  1441.7 38.5 all-reduce.13
  1674.6 51.6 all-reduce.15
where the time goes:
time: 1750 us; the launch traced here: 1740 us
  waiting for transfers between devices  595 us (34%)
  blocking collectives  376 us (21%)
  other arithmetic  298 us (17%)
  local copies, waits for them, and re-layouts  279 us (16%)
  matrix products  173 us (10%)
    psum x2, waiting for transfers between devices, find_basis(): panel = lax.psum(sketch_term(blocks, right), 'col')  400 us
    all_to_all x1, blocking collectives, local(): lax.all_to_all(delta, 'col', split_axis=2, concat_axis=1, tiled=True)  376 us
    another operation x17, other arithmetic, orthonormal(): lower = jnp.linalg.cholesky(gram_total)  134 us
    convert_element_type x1, local copies, waits for them, and re-layouts, local(): (adjusted_flat.astype(jnp.float32) - base_flat.astype(jnp.float32)).astyp...  82 us
    all_to_all x1, local copies, waits for them, and re-layouts, local(): lax.all_to_all(delta, 'col', split_axis=2, concat_axis=1, tiled=True)  80.7 us
    another operation x6, other arithmetic, orthonormal(): solved = jax.scipy.linalg.solve_triangular(lower, stacked, lower=True)  79 us
    psum x2, waiting for transfers between devices, find_basis(): gram_total = lax.psum(gram_of(panel, matrix_list, adapter_rank), 'row')  77.2 us
    dot_general x2, matrix products, gram_of(): jnp.einsum('rmk,rml->mkl', panel_three, panel_three, precision=lax.Precis...  61.9 us
  transfers between devices with their start and end apart: 7, of which 7 were waited for; matrix products, arithmetic and copies ran while one was open for 0% of the time, Pallas kernels for 0%

commit v1 on v0

--- a/solution.py
+++ b/solution.py
@@ -47,7 +47,10 @@
     matrix_list = base_flat.shape[0]
     adapter_rank = omega.shape[2]
     delta = (adjusted_flat.astype(jnp.float32) - base_flat.astype(jnp.float32)).astype(jnp.bfloat16)
-    blocks = lax.all_to_all(delta, "col", split_axis=2, concat_axis=1, tiled=True)
+    size = lax.axis_size("col")
+    shards = jnp.stack(jnp.split(delta, size, axis=2), axis=0)
+    shards = lax.all_to_all(shards, "col", split_axis=0, concat_axis=0)
+    blocks = jnp.concatenate(shards, axis=1)
     block_rows = blocks.shape[1]
     block_cols = blocks.shape[2]
     segment_rows = block_rows // lax.axis_size("col")

time: 1750 us -> 2160 us (1.23)
  local copies, waits for them, and re-layouts: 279 us -> 721 us
  blocking collectives: 376 us -> 340 us
    slice x1 -> x2, local copies, waits for them, and re-layouts: 21.5 us -> 574 us  [sketch_term(): rows = blocks[index]]
    convert_element_type x1 -> x0, local copies, waits for them, and re-layouts: 82 us -> none  [local(): (adjusted_flat.astype(jnp.float32) - base_flat.astype(jnp.float32)).astyp...]
    all_to_all x1 -> x0, local copies, waits for them, and re-layouts: 80.7 us -> none  [local(): lax.all_to_all(delta, 'col', split_axis=2, concat_axis=1, tiled=True)]
    unnamed x30 -> x37, local copies, waits for them, and re-layouts: 7.39 us -> 53.4 us
    all_to_all x1, blocking collectives: 376 us -> 340 us  [local(): shards = lax.all_to_all(shards, 'col', split_axis=0, concat_axis=0)]
where the time goes in v1:
time: 2160 us; the launch traced here: 2150 us
  local copies, waits for them, and re-layouts  721 us (33%)
  waiting for transfers between devices  595 us (28%)
  blocking collectives  340 us (16%)
  other arithmetic  306 us (14%)
  matrix products  173 us (8%)
    slice x2, local copies, waits for them, and re-layouts, sketch_term(): rows = blocks[index]  574 us
    psum x2, waiting for transfers between devices, find_basis(): panel = lax.psum(sketch_term(blocks, right), 'col')  400 us
    all_to_all x1, blocking collectives, local(): shards = lax.all_to_all(shards, 'col', split_axis=0, concat_axis=0)  340 us
    another operation x17, other arithmetic, orthonormal(): lower = jnp.linalg.cholesky(gram_total)  134 us
    another operation x6, other arithmetic, orthonormal(): solved = jax.scipy.linalg.solve_triangular(lower, stacked, lower=True)  79 us
    psum x2, waiting for transfers between devices, find_basis(): gram_total = lax.psum(gram_of(panel, matrix_list, adapter_rank), 'row')  77.2 us
    dot_general x2, matrix products, gram_of(): jnp.einsum('rmk,rml->mkl', panel_three, panel_three, precision=lax.Precis...  61.9 us
    unnamed x37, local copies, waits for them, and re-layouts  53.4 us
  transfers between devices with their start and end apart: 7, of which 7 were waited for; matrix products, arithmetic and copies ran while one was open for 0% of the time, Pallas kernels for 0%

profile of v1, /device:TPU:0, one launch (start us, length us, event | category | flops | bytes accessed | tf_op | source)
XLA Modules:
  0.0 2150.3 jit_solution(13536002849445281)
XLA Ops:
  7.2 39.5 %subtract_convert_fusion = bf16[2,924,8192]{2,0,1:T(2,128)(2,1)} fusion(bf16[2,924,8192]{2,0,1:T(2,128)(2,1)} %param.6, bf16[2,924,8192]{2,0,1:T(2,128)(2,1)} %param.7), kind=kLoop, calls=%fused_computation.4 | loop fusion | flops 60555264 | bytes 90832896 | tf_op jit(solution)/shard_map/convert_element_type | solution.py:49
  99.3 339.8 %all_to_all.5 = bf16[8,2,924,1024]{3,1,2,0:T(2,128)(2,1)} all-to-all(bf16[8,2,924,1024]{3,1,2,0:T(2,128)(2,1)} %fusion.13), channel_id=1, replica_groups=mesh['row'=4,'col'=8] {'col'}, dimensions={0} | all-to-all | bytes 60555264 | tf_op jit(solution)/shard_map/all_to_all | solution.py:52
  439.1 268.8 %slice_reduce_fusion = bf16[8,924,1024]{2,1,0:T(8,128)(2,1)} fusion(bf16[2,8,924,1024]{3,0,2,1:T(2,128)(2,1)} %bitcast.157), kind=kLoop, calls=%fused_computation.5 | loop fusion | bytes 30277632 | tf_op jit(solution)/shard_map/slice | solution.py:13
  707.9 305.5 %slice_reduce_fusion.1 = bf16[8,924,1024]{2,1,0:T(8,128)(2,1)} fusion(bf16[2,8,924,1024]{3,0,2,1:T(2,128)(2,1)} %bitcast.158), kind=kLoop, calls=%fused_computation.6 | loop fusion | bytes 30277632 | tf_op jit(solution)/shard_map/slice | solution.py:13
  1013.4 11.4 squeeze.26
  1024.8 11.6 squeeze.24
  1052.4 9.5 pad_maximum_fusion
  1061.9 11.9 copy.109
  1073.9 200.5 %all-reduce.8.cloned.1.call-done = f32[7392,2,256]{2,0,1:T(8,128)} async-done(((f32[7392,2,256]{2,0,1:T(8,128)}), f32[7392,2,256]{2,0,1:T(8,128)}) %all-reduce.8.cloned.1.call-update) | async-done | bytes 15138832 | tf_op jit(solution)/shard_map/psum | solution.py:61
  1274.4 31.0 %fusion.61 = f32[2,256,256]{1,2,0:T(8,128)} fusion(f32[7392,2,256]{2,0,1:T(8,128)} %all-reduce.8.cloned.1.call-done), kind=kOutput, calls=%fused_computation.107 | convolution fusion | flops 11626610688 | bytes 15663104 | tf_op jit(solution)/shard_map/rmk,rml->mkl/dot_general | solution.py:20
  1305.5 38.6 %all-reduce.10.cloned.1.call-done = f32[2,256,256]{1,2,0:T(8,128)} async-done(((f32[2,256,256]{1,2,0:T(8,128)}), f32[2,256,256]{1,2,0:T(8,128)}) %all-reduce.10.cloned.1.call-update) | async-done | bytes 524304 | tf_op jit(solution)/shard_map/psum | solution.py:62
  1346.5 23.5 %custom-call.17 = f32[2,128,128]{2,1,0:T(8,128)S(1)} custom-call(f32[2,128,128]{2,1,0:T(8,128)S(1)} %cholesky.198), custom_call_target="Cholesky" | custom-call | tf_op jit(solution)/shard_map/jit(cholesky)/cholesky | solution.py:24
  1370.0 19.7 custom-call.18
  1390.4 23.5 %custom-call.19 = f32[2,128,128]{2,1,0:T(8,128)S(1)} custom-call(f32[2,128,128]{2,1,0:T(8,128)S(1)} %convolution_subtract_fusion.3), custom_call_target="Cholesky" | custom-call | tf_op jit(solution)/shard_map/jit(cholesky)/cholesky | solution.py:24
  1418.1 39.3 %custom-call.20 = f32[2,2,128,128]{2,3,1,0:T(8,128)S(1)} custom-call(f32[2,2,128,128]{3,2,1,0:T(8,128)S(1)} %bitcast.175), custom_call_target="InvertDiagBlocksLowerTriangular" | custom-call | tf_op jit(solution)/shard_map/jit(_solve_triangular)/vmap()/triangular_solve | solution.py:26
  1488.9 10.2 copy.71
  1517.7 43.5 %reduce-scatter.2.cloned.1.call-done = f32[2,256,256]{2,1,0:T(8,128)} async-done(((f32[2,1024,256]{2,1,0:T(8,128)}), f32[2,256,256]{2,1,0:T(8,128)}) %reduce-scatter.2.cloned.1.call-update) | async-done | bytes 524304 | tf_op jit(solution)/shard_map/reduce_scatter | solution.py:69
  1563.1 27.4 %all-gather.2.cloned.1.call-done = bf16[2,1024,256]{2,1,0:T(8,128)(2,1)} async-done(((bf16[2,256,256]{2,1,0:T(8,128)(2,1)}), bf16[2,1024,256]{2,1,0:T(8,128)(2,1)}) %all-gather.2.cloned.1.call-update) | async-done | bytes 1048592 | tf_op jit(solution)/shard_map/all_gather | solution.py:70
  1590.4 9.8 fusion.40
  1613.8 11.9 copy.108
  1625.7 199.8 %all-reduce.12.cloned.1.call-done = f32[7392,2,256]{2,0,1:T(8,128)} async-done(((f32[7392,2,256]{2,0,1:T(8,128)}), f32[7392,2,256]{2,0,1:T(8,128)}) %all-reduce.12.cloned.1.call-update) | async-done | bytes 15138832 | tf_op jit(solution)/shard_map/psum | solution.py:61
  1825.6 30.9 %fusion.62 = f32[2,256,256]{1,2,0:T(8,128)} fusion(f32[7392,2,256]{2,0,1:T(8,128)} %all-reduce.12.cloned.1.call-done), kind=kOutput, calls=%fused_computation.108 | convolution fusion | flops 11626610688 | bytes 15663104 | tf_op jit(solution)/shard_map/rmk,rml->mkl/dot_general | solution.py:20
  1856.5 38.7 %all-reduce.14.cloned.1.call-done = f32[2,256,256]{1,2,0:T(8,128)} async-done(((f32[2,256,256]{1,2,0:T(8,128)}), f32[2,256,256]{1,2,0:T(8,128)}) %all-reduce.14.cloned.1.call-update) | async-done | bytes 524304 | tf_op jit(solution)/shard_map/psum | solution.py:62
  1897.6 23.5 %custom-call.21 = f32[2,128,128]{2,1,0:T(8,128)S(1)} custom-call(f32[2,128,128]{2,1,0:T(8,128)S(1)} %cholesky.201), custom_call_target="Cholesky" | custom-call | tf_op jit(solution)/shard_map/jit(cholesky)/cholesky | solution.py:24
  1921.1 19.7 custom-call.22
  1941.5 23.5 %custom-call.23 = f32[2,128,128]{2,1,0:T(8,128)S(1)} custom-call(f32[2,128,128]{2,1,0:T(8,128)S(1)} %convolution_subtract_fusion.2), custom_call_target="Cholesky" | custom-call | tf_op jit(solution)/shard_map/jit(cholesky)/cholesky | solution.py:24
  1969.3 39.3 %custom-call.24 = f32[2,2,128,128]{2,3,1,0:T(8,128)S(1)} custom-call(f32[2,2,128,128]{3,2,1,0:T(8,128)S(1)} %bitcast.174), custom_call_target="InvertDiagBlocksLowerTriangular" | custom-call | tf_op jit(solution)/shard_map/jit(_solve_triangular)/vmap()/triangular_solve | solution.py:26
  2032.3 11.6 maximum_bitcast_fusion
  2044.0 15.4 copy.80
  2059.4 9.1 bitcast_convert_fusion
  2068.5 10.7 fusion.36
  2095.1 46.1 %all-reduce.16.cloned.1.call-done = bf16[2,1024,256]{1,0,2:T(2,128)(2,1)} async-done(((bf16[2,1024,256]{1,0,2:T(2,128)(2,1)}), bf16[2,1024,256]{1,0,2:T(2,128)(2,1)}) %all-reduce.16.cloned.1.call-update) | async-done | bytes 1048592
  (118 shorter events, 197.8 us)
Async XLA Ops:
  7.2 1267.2 %all-reduce.8.cloned.1.call-start = ((), (), s32[]{:S(2)}) async-start(), calls=%async_computation.2 | async-start | bytes 30277632 | tf_op jit(solution)/shard_map/psum | solution.py:61
  1024.8 11.6 copy-start.7
  1036.3 9.6 copy-start.4
  1073.8 270.3 %all-reduce.10.cloned.1.call-start = ((), (), s32[]{:S(2)}) async-start(), calls=%async_computation.3 | async-start | bytes 1048576 | tf_op jit(solution)/shard_map/psum | solution.py:62
  1305.4 255.8 %reduce-scatter.2.cloned.1.call-start = ((), (), s32[]{:S(2)}) async-start(), calls=%async_computation.4 | async-start | bytes 2621440 | tf_op jit(solution)/shard_map/reduce_scatter | solution.py:69
  1457.5 8.9 copy-start
  1466.4 6.7 copy-start.2
  1499.1 9.0 slice-start
  1499.1 9.8 copy-start.6
  1499.1 11.0 slice-start.1
  1499.1 12.2 slice-start.2
  1499.1 12.9 slice-start.3
  1517.7 72.8 %all-gather.2.cloned.1.call-start = ((), (), s32[]{:S(2)}) async-start(), calls=%async_computation.5 | async-start | bytes 1310720 | tf_op jit(solution)/shard_map/all_gather | solution.py:70
  1563.0 262.5 %all-reduce.12.cloned.1.call-start = ((), (), s32[]{:S(2)}) async-start(), calls=%async_computation.6 | async-start | bytes 30277632 | tf_op jit(solution)/shard_map/psum | solution.py:61
  1590.4 9.8 copy-start.8
  1625.7 269.5 %all-reduce.14.cloned.1.call-start = ((), (), s32[]{:S(2)}) async-start(), calls=%async_computation.7 | async-start | bytes 1048576 | tf_op jit(solution)/shard_map/psum | solution.py:62
  1856.5 284.7 %all-reduce.16.cloned.1.call-start = ((), (), s32[]{:S(2)}) async-start(), calls=%async_computation.8 | async-start | bytes 2097152
  2008.6 8.9 copy-start.1
  2017.5 6.7 copy-start.3
  2068.5 10.7 copy-start.5
  2079.2 10.2 copy-start.9
Sparse Core Ops, SparseCore 0:
  1073.9 200.4 all-reduce.7
  1305.5 38.5 all-reduce.9
  1517.8 43.3 reduce-scatter.1
  1563.2 27.1 all-gather.1
  1625.8 199.7 all-reduce.11
  1856.6 38.5 all-reduce.13
  2089.5 51.7 all-reduce.15
